TPU v7x, 32 devices: a whole 2x2x4 slice. The times are simulated.
32 devices in a mesh: leaf: 16 (over z, y, x), col: 2 (over core).
Axes of the slice: x: 2, y: 2, z: 4, core: 2. Of those that a mesh axis runs over, the one named last changes fastest.
Arguments:
- sources: bfloat16 [65536, 256], P('leaf', 'col'), may hold values from -6 to 6
- near_tiles: bfloat16 [256, 8, 256, 256], P('leaf', 'col'), may hold values from -0.125 to 0.125
- near_index: int32 [256, 8], P('leaf'), may hold values from 0 to 255, as said below
- near_count: int32 [256], P('leaf'), may hold values from 1 to 8, as said below
- leaf_basis: bfloat16 [256, 64, 256], P('leaf'), may hold values from -0.375 to 0.375
- leaf_coupling: bfloat16 [256, 64, 256], P('leaf'), may hold values from -0.375 to 0.375
- leaf_far: int32 [256, 4], P('leaf'), may hold values from 0 to 255, as said below
- up_leaf: bfloat16 [32, 64, 512], P('leaf'), may hold values from -0.25 to 0.25
- mid_coupling: bfloat16 [32, 64, 256], P('leaf'), may hold values from -0.375 to 0.375
- mid_far: int32 [32, 4], P('leaf'), may hold values from 0 to 31, as said below
- up_mid: bfloat16 [32, 64, 64], P('leaf'), may hold values from -0.75 to 0.75
- top_coupling: bfloat16 [4, 64, 256], replicated, may hold values from -0.4375 to 0.4375
Outputs:
- product: float32 [65536, 256], P('leaf', 'col')
Inputs may be any that keep to these rules, and one draw needn't show every extreme that they name: `near_index`: entry 0 of row i is i; the other 7 entries are distinct leaves j with j != i and |i - j| <= 8. Only the first near_count[i] slots of leaf i count; some leaf has all 8. `leaf_far`: row i holds 4 distinct leaves j != i with |i // 8 - j // 8| <= 1. `mid_far`: row a holds 4 distinct middle clusters b != a with |a // 8 - b // 8| <= 1.
All inputs are finite; a program needn't handle non-finite values.
Results may differ from a plain program's by a relative error of at most 0.01.
Values may be sent and summed in bfloat16 or wider, within the bound.
No kernel may reach another device: no remote copies, remote signals or barrier semaphores. Data moves between devices by JAX's collectives and lax.ppermute only.
A program may use at most 128 MiB of HBM per device.

v0:
```python
import jax
import jax.numpy as jnp
from jax import lax
from jax.sharding import PartitionSpec as P

CHILD = 8
FAR = 4


def padded(x, sides, width):
    for axis, dim in sides:
        size, length = (lax.axis_size(axis), x.shape[dim])
        up = [(i, (i + 1) % size) for i in range(size - 1)]
        down = [(j, i) for i, j in up]
        last = lax.slice_in_dim(x, length - width, length, axis=dim)
        first = lax.slice_in_dim(x, 0, width, axis=dim)
        before = lax.ppermute(last, axis, up)
        after = lax.ppermute(first, axis, down)
        x = jnp.concatenate([before, x, after], axis=dim)
    return x


def shards(
    sources,
    near_tiles,
    near_index,
    near_count,
    leaf_basis,
    leaf_coupling,
    leaf_far,
    up_leaf,
    mid_coupling,
    mid_far,
    up_mid,
    top_coupling,
):
    f32 = jnp.float32
    bf16 = jnp.bfloat16
    leaf_count = leaf_basis.shape[0]
    rank_size = leaf_basis.shape[1]
    leaf_size = leaf_basis.shape[2]
    col_count = sources.shape[1]
    mid_count = leaf_count // CHILD
    total_top = top_coupling.shape[0]
    device = lax.axis_index("leaf")
    first_leaf = device * leaf_count
    first_mid = device * mid_count
    window = padded(sources, (("leaf", 0),), CHILD * leaf_size)
    near_local = near_index - (first_leaf - CHILD)
    all_tiles = lax.all_gather(near_tiles, "col", axis=1, tiled=True)
    slot_count = all_tiles.shape[1]
    blocks = window.reshape(-1, leaf_size, window.shape[1])
    picked = blocks[near_local]
    live_mask = jnp.arange(slot_count)[None, :] < near_count[:, None]
    picked = jnp.where(live_mask[:, :, None, None], picked, jnp.zeros((), bf16))
    result = jnp.einsum("lsij,lsjc->lic", all_tiles, picked, preferred_element_type=f32)
    near_part = result.reshape(leaf_count * leaf_size, window.shape[1])
    leaf_blocks = sources.reshape(leaf_count, leaf_size, col_count)
    leaf_coef = jnp.einsum(
        "lrk,lkc->lrc", leaf_basis, leaf_blocks, preferred_element_type=f32
    ).astype(bf16)
    mid_coef = jnp.einsum(
        "qrk,qkc->qrc",
        up_leaf,
        leaf_coef.reshape(mid_count, CHILD * rank_size, col_count),
        preferred_element_type=f32,
    ).astype(bf16)
    mid_lift = jnp.einsum("qrs,qsc->qrc", up_mid, mid_coef, preferred_element_type=f32).astype(bf16)
    parent = (first_mid + jnp.arange(mid_count)) // CHILD
    mid_flat = mid_far.reshape(-1)
    top_range = jnp.arange(total_top)
    coef_piece = lax.all_gather(mid_coef, "leaf", axis=0, tiled=True)
    lift_piece = lax.all_gather(mid_lift, "leaf", axis=0, tiled=True)
    global_ids = jnp.arange(coef_piece.shape[0])
    group_map = (top_range[:, None] == (global_ids // CHILD)[None, :]).astype(bf16)
    top_total = jnp.einsum("pk,krc->prc", group_map, lift_piece, preferred_element_type=f32)
    global_ids = jnp.arange(coef_piece.shape[0])
    pick_map = (mid_flat[:, None] == global_ids[None, :]).astype(bf16)
    mid_picked = jnp.einsum("ik,krc->irc", pick_map, coef_piece, preferred_element_type=f32)
    top_coef = top_total.astype(bf16)
    parent_rows = top_coupling[parent]
    keep_mask = top_range[None, :] != parent[:, None]
    stacked = jnp.where(keep_mask[:, :, None, None], top_coef[None], jnp.zeros((), bf16))
    top_field = jnp.einsum(
        "qrk,qkc->qrc",
        parent_rows,
        stacked.reshape(mid_count, total_top * rank_size, col_count),
        preferred_element_type=f32,
    ).astype(bf16)
    mid_chosen = mid_picked.astype(bf16).reshape(mid_count, FAR * rank_size, col_count)
    mid_field = (
        jnp.einsum("qrk,qkc->qrc", mid_coupling, mid_chosen, preferred_element_type=f32)
        + jnp.einsum("qrs,qrc->qsc", up_mid, top_field, preferred_element_type=f32)
    ).astype(bf16)
    leaf_window = padded(leaf_coef, (("leaf", 0),), CHILD)
    far_local = leaf_far - (first_leaf - CHILD)
    leaf_chosen = leaf_window[far_local].reshape(leaf_count, FAR * rank_size, col_count)
    down_part = jnp.einsum("qrs,qrc->qsc", up_leaf, mid_field, preferred_element_type=f32).reshape(
        leaf_count, rank_size, col_count
    )
    leaf_field = (
        jnp.einsum("lrk,lkc->lrc", leaf_coupling, leaf_chosen, preferred_element_type=f32)
        + down_part
    ).astype(bf16)
    far_part = jnp.einsum(
        "lrk,lrc->lkc", leaf_basis, leaf_field, preferred_element_type=f32
    ).reshape(leaf_count * leaf_size, col_count)
    return near_part + far_part


def solution(mesh):
    return jax.shard_map(
        shards,
        mesh=mesh,
        in_specs=(
            P("leaf", "col"),
            P("leaf", "col", None, None),
            P("leaf", None),
            P("leaf"),
            P("leaf", None, None),
            P("leaf", None, None),
            P("leaf", None),
            P("leaf", None, None),
            P("leaf", None, None),
            P("leaf", None),
            P("leaf", None, None),
            P(),
        ),
        out_specs=P("leaf", "col"),
        check_vma=False,
    )
```

profile of v0, /device:TPU:0, one launch (start us, length us, event | category | flops | bytes accessed | tf_op | source)
XLA Modules:
  0.0 168.7 jit_solution(13844385451105794318)
XLA Ops:
  6.5 0.7 all-gather.2.cloned.1.call-update
  7.3 0.0 copy-start.9
  7.3 0.0 copy-start.4
  7.3 0.0 copy-start.6
  7.3 0.0 copy-start.11
  7.3 0.0 copy-start.7
  7.3 0.0 copy-start.10
  7.3 0.2 copy-done
  7.6 0.3 copy-done.1
  7.9 0.3 convolution_convert_fusion
  8.3 4.9 %collective-permute-start.2 = (bf16[8,64,128]{2,1,0:T(8,128)(2,1)S(1)}, bf16[8,64,128]{2,1,0:T(8,128)(2,1)S(1)}, u32[]{:S(2)}, u32[]{:S(2)}) collective-permute-start(bf16[8,64,128]{2,1,0:T(8,128)(2,1)S(1)} %get-tuple-element.7), channel_id=1, source_target_pairs={{0,2},{2,4},{4,6},{6,8},{8,10},{10,12},{12,14},{14,16},{16,18},{18... | collective-permute-start | bytes 393224 | tf_op jit(solution)/shard_map/ppermute | solution.py:17
  13.2 1.3 collective-permute-start.3
  14.5 1.1 fusion.33
  15.5 5.4 %collective-permute-start = (bf16[2048,128]{1,0:T(8,128)(2,1)}, bf16[2048,128]{1,0:T(8,128)(2,1)}, u32[]{:S(2)}, u32[]{:S(2)}) collective-permute-start(bf16[2048,128]{1,0:T(8,128)(2,1)} %get-tuple-element.5), channel_id=1, source_target_pairs={{0,2},{2,4},{4,6},{6,8},{8,10},{10,12},{12,14},{14,16},{16,18},{18... | collective-permute-start | bytes 1572872 | tf_op jit(solution)/shard_map/ppermute | solution.py:17
  20.9 1.3 collective-permute-start.1
  22.2 0.1 copy.27
  22.3 0.1 reshape.160
  22.4 0.2 convolution_convert_fusion.5
  22.6 0.1 fusion.12
  22.7 0.0 copy-start.3
  22.7 57.8 %all_gather.11 = bf16[32,64,128]{2,1,0:T(8,128)(2,1)S(1)} all-gather(bf16[2,64,128]{2,1,0:T(8,128)(2,1)S(1)} %fusion.12), channel_id=1, replica_groups=mesh['leaf'=16,'col'=2] {'leaf'}, dimensions={0}, use_global_device_ids=true | all-gather | bytes 557056 | tf_op jit(solution)/shard_map/all_gather | solution.py:73
  80.5 0.4 convolution_convert_fusion.2
  80.9 0.1 iota_compare_fusion.3
  81.0 0.1 broadcast_in_dim.59
  81.1 0.1 broadcast_in_dim.60
  81.2 0.1 eq.28
  81.3 38.7 %all_gather.10 = bf16[32,64,128]{2,1,0:T(8,128)(2,1)S(1)} all-gather(bf16[2,64,128]{2,1,0:T(8,128)(2,1)S(1)} %bitcast.59), channel_id=1, replica_groups=mesh['leaf'=16,'col'=2] {'leaf'}, dimensions={0}, use_global_device_ids=true | all-gather | bytes 557056 | tf_op jit(solution)/shard_map/all_gather | solution.py:72
  119.9 0.4 convolution_convert_fusion.1
  120.4 0.6 gather_fusion.2
  121.0 0.1 iota_compare_fusion
  121.1 0.4 fusion.11
  121.5 0.0 copy-done.5
  121.5 0.4 convolution_bitcast_fusion.1
  121.9 0.1 copy.25
  122.0 0.1 reshape.152
  122.1 0.2 copy.33
  122.3 0.0 collective-permute-done.2
  122.3 0.0 collective-permute-done.3
  122.3 1.0 pad_maximum_fusion.1
  123.3 0.7 gather_fusion.1
  124.0 1.9 %fusion.9 = f32[16,128,256]{2,1,0:T(8,128)} fusion(bf16[16,64,256]{2,1,0:T(8,128)(2,1)S(1)} %copy-done, f32[16,64,128]{2,1,0:T(8,128)S(1)} %bitcast.57, bf16[16,64,256]{2,1,0:T(8,128)(2,1)S(1)} %copy-done.3, bf16[16,256,128]{2,1,0:T(8,128)(2,1)S(1)} %bitcast.56), kind=kOutput, calls=%fused_computation.15 | convolution fusion | flops 134479872 | bytes 4718592 | tf_op jit(solution)/shard_map/lrk,lrc->lkc/dot_general | solution.py:105
  126.0 0.0 collective-permute-done
  126.0 0.0 collective-permute-done.1
  126.0 1.7 pad_maximum_fusion
  127.6 6.6 %gather_fusion = bf16[128,256,128]{2,1,0:T(8,128)(2,1)} fusion(bf16[32,256,128]{2,1,0:T(8,128)(2,1)S(1)} %bitcast.52, s32[1024]{0:T(1024)S(1)} %pad_clamp_fusion.2), kind=kCustom, calls=%fused_computation | custom fusion | bytes 16777728 | tf_op jit(solution)/shard_map/gather | solution.py:53
  134.2 12.1 %copy.26 = bf16[128,256,128]{1,2,0:T(8,128)(2,1)} copy(bf16[128,256,128]{2,1,0:T(8,128)(2,1)} %gather_fusion) | data formatting | bytes 16777216 | tf_op jit(solution)/shard_map/gather | solution.py:53
  146.3 12.7 %fusion.4 = f32[16,256,128]{1,2,0:T(8,128)} fusion(f32[16,128,256]{2,1,0:T(8,128)S(1)} %copy-done.2, bf16[16,8,256,256]{3,2,1,0:T(8,128)(2,1)} %all-gather.2.cloned.1.call-done, bf16[16,8,256,128]{2,3,1,0:T(8,128)(2,1)} %bitcast.54, pred[16,8]{1,0:T(8,128)(4,1)S(1)} %iota_compare_fusion), kind=kOutput, calls=%fused_computation.9 | convolution fusion | flops 2152202240 | bytes 29360256 | tf_op jit(solution)/shard_map/lsij,lsjc->lic/dot_general | solution.py:56
  159.0 2.9 %copy.34 = f32[16,256,128]{2,1,0:T(8,128)} copy(f32[16,256,128]{1,2,0:T(8,128)} %fusion.4) | data formatting | bytes 4194304 | tf_op jit(solution)/shard_map/add | solution.py:108
  (27 shorter events, 0.2 us)
Async XLA Ops:
  6.5 1.0 copy-start
  6.5 1.4 copy-start.1
  6.5 139.8 %all-gather.2.cloned.1.call-start = ((), (), s32[]{:S(2)}) async-start(), calls=%async_computation | async-start | bytes 25165824 | tf_op jit(solution)/shard_map/all_gather | solution.py:50
  7.3 14.9 %copy-start.9 = (s32[16,4]{0,1:T(4,128)S(1)}, s32[16,4]{0,1:T(4,128)}, u32[]{:S(2)}) copy-start(s32[16,4]{0,1:T(4,128)} %param.18) | copy-start | bytes 772
  7.3 15.1 %copy-start.4 = (bf16[2,64,512]{2,1,0:T(8,128)(2,1)S(1)}, bf16[2,64,512]{2,1,0:T(8,128)(2,1)}, u32[]{:S(2)}) copy-start(bf16[2,64,512]{2,1,0:T(8,128)(2,1)} %param.19) | copy-start | bytes 393220
  7.3 15.3 %copy-start.6 = (bf16[2,64,64]{2,1,0:T(8,128)(2,1)S(1)}, bf16[2,64,64]{2,1,0:T(8,128)(2,1)}, u32[]{:S(2)}) copy-start(bf16[2,64,64]{2,1,0:T(8,128)(2,1)} %param.22) | copy-start | bytes 49156
  7.3 73.9 %copy-start.11 = (s32[2,4]{1,0:T(2,128)S(1)}, s32[2,4]{1,0:T(2,128)}, u32[]{:S(2)}) copy-start(s32[2,4]{1,0:T(2,128)} %param.21) | copy-start | bytes 100
  7.3 113.1 %copy-start.7 = (bf16[4,64,256]{2,1,0:T(8,128)(2,1)S(1)}, bf16[4,64,256]{2,1,0:T(8,128)(2,1)}, u32[]{:S(2)}) copy-start(bf16[4,64,256]{2,1,0:T(8,128)(2,1)} %param.23) | copy-start | bytes 393220
  7.3 113.7 %copy-start.10 = (s32[16]{0:T(128)S(1)}, s32[16]{0:T(128)}, u32[]{:S(2)}) copy-start(s32[16]{0:T(128)} %param.15) | copy-start | bytes 196
  7.3 113.7 %copy-start.8 = (s32[16,8]{0,1:T(8,128)S(1)}, s32[16,8]{0,1:T(8,128)}, u32[]{:S(2)}) copy-start(s32[16,8]{0,1:T(8,128)} %param.14) | copy-start | bytes 1540
  7.3 114.1 %copy-start.5 = (bf16[2,64,256]{2,1,0:T(8,128)(2,1)S(1)}, bf16[2,64,256]{2,1,0:T(8,128)(2,1)}, u32[]{:S(2)}) copy-start(bf16[2,64,256]{2,1,0:T(8,128)(2,1)} %param.20) | copy-start | bytes 196612
  8.3 114.0 %collective-permute-start.2 = (bf16[8,64,128]{2,1,0:T(8,128)(2,1)S(1)}, bf16[8,64,128]{2,1,0:T(8,128)(2,1)S(1)}, u32[]{:S(2)}, u32[]{:S(2)}) collective-permute-start(bf16[8,64,128]{2,1,0:T(8,128)(2,1)S(1)} %get-tuple-element.7), channel_id=1, source_target_pairs={{0,2},{2,4},{4,6},{6,8},{8,10},{10,12},{12,14},{14,16},{16,18},{18... | collective-permute-start | bytes 393224 | tf_op jit(solution)/shard_map/ppermute | solution.py:17
  13.2 109.1 %collective-permute-start.3 = (bf16[8,64,128]{2,1,0:T(8,128)(2,1)S(1)}, bf16[8,64,128]{2,1,0:T(8,128)(2,1)}, u32[]{:S(2)}, u32[]{:S(2)}) collective-permute-start(bf16[8,64,128]{2,1,0:T(8,128)(2,1)S(1)} %get-tuple-element.8), channel_id=1, source_target_pairs={{2,0},{4,2},{6,4},{8,6},{10,8},{12,10},{14,12},{16,14},{18,16},{20... | collective-permute-start | bytes 393224 | tf_op jit(solution)/shard_map/ppermute | solution.py:18
  15.5 110.4 %collective-permute-start = (bf16[2048,128]{1,0:T(8,128)(2,1)}, bf16[2048,128]{1,0:T(8,128)(2,1)}, u32[]{:S(2)}, u32[]{:S(2)}) collective-permute-start(bf16[2048,128]{1,0:T(8,128)(2,1)} %get-tuple-element.5), channel_id=1, source_target_pairs={{0,2},{2,4},{4,6},{6,8},{8,10},{10,12},{12,14},{14,16},{16,18},{18... | collective-permute-start | bytes 1572872 | tf_op jit(solution)/shard_map/ppermute | solution.py:17
  20.9 105.1 %collective-permute-start.1 = (bf16[2048,128]{1,0:T(8,128)(2,1)}, bf16[2048,128]{1,0:T(8,128)(2,1)}, u32[]{:S(2)}, u32[]{:S(2)}) collective-permute-start(bf16[2048,128]{1,0:T(8,128)(2,1)} %get-tuple-element.6), channel_id=1, source_target_pairs={{2,0},{4,2},{6,4},{8,6},{10,8},{12,10},{14,12},{16,14},{18,16},{20... | collective-permute-start | bytes 1572872 | tf_op jit(solution)/shard_map/ppermute | solution.py:18
  22.7 101.3 %copy-start.3 = (bf16[16,64,256]{2,1,0:T(8,128)(2,1)S(1)}, bf16[16,64,256]{2,1,0:T(8,128)(2,1)}, u32[]{:S(2)}) copy-start(bf16[16,64,256]{2,1,0:T(8,128)(2,1)} %param.17) | copy-start | bytes 1572868
  134.2 12.1 %copy-start.2 = (f32[16,128,256]{2,1,0:T(8,128)S(1)}, f32[16,128,256]{2,1,0:T(8,128)}, u32[]{:S(2)}) copy-start(f32[16,128,256]{2,1,0:T(8,128)} %fusion.9) | copy-start | bytes 6291460
Sparse Core Ops, SparseCore 0:
  8.9 32.7 all-gather.1
where the time goes:
time: 169 us
  blocking collectives  96.5 us (57%)
  local copies, waits for them, and re-layouts  25.4 us (15%)
  matrix products  16.8 us (10%)
  between operations  13.7 us (8%)
  starting transfers between devices  12.8 us (8%)
  other arithmetic  2.82 us (2%)
    all_gather x1, blocking collectives, shards(): lift_piece = lax.all_gather(mid_lift, 'leaf', axis=0, tiled=True)  57.8 us
    all_gather x1, blocking collectives, shards(): coef_piece = lax.all_gather(mid_coef, 'leaf', axis=0, tiled=True)  38.7 us
    gather x2, local copies, waits for them, and re-layouts, shards(): picked = blocks[near_local]  18.7 us
    dot_general x1, matrix products, shards(): jnp.einsum('lsij,lsjc->lic', all_tiles, picked, preferred_element_type=f32)  12.7 us
    ppermute x2, starting transfers between devices, padded(): before = lax.ppermute(last, axis, up)  10.2 us
  transfers between devices with their start and end apart: 5, of which 0 were waited for; matrix products, arithmetic and copies ran while one was open for 17% of the time, Pallas kernels for 0%

commit v1 on v0

--- a/solution.py
+++ b/solution.py
@@ -5,6 +5,18 @@
 
 CHILD = 8
 FAR = 4
+
+
+def product_in_turn(array, axis, dim, product):
+    length, index, rows = (lax.axis_size(axis), lax.axis_index(axis), array.shape[dim])
+    right = [(i, (i + 1) % length) for i in range(length)]
+    held, total = (array, None)
+    for step in range(length):
+        arriving = lax.ppermute(held, axis, right) if step < length - 1 else None
+        update = product(held, (index - step) % length * rows)
+        total = update if total is None else total + update
+        held = arriving
+    return total
 
 
 def padded(x, sides, width):
@@ -70,10 +82,19 @@
     mid_flat = mid_far.reshape(-1)
     top_range = jnp.arange(total_top)
     coef_piece = lax.all_gather(mid_coef, "leaf", axis=0, tiled=True)
-    lift_piece = lax.all_gather(mid_lift, "leaf", axis=0, tiled=True)
     global_ids = jnp.arange(coef_piece.shape[0])
     group_map = (top_range[:, None] == (global_ids // CHILD)[None, :]).astype(bf16)
-    top_total = jnp.einsum("pk,krc->prc", group_map, lift_piece, preferred_element_type=f32)
+    top_total = product_in_turn(
+        mid_lift,
+        "leaf",
+        0,
+        lambda own_block, offset: jnp.einsum(
+            "pk,krc->prc",
+            lax.dynamic_slice_in_dim(group_map, offset, own_block.shape[0], axis=1),
+            own_block,
+            preferred_element_type=f32,
+        ),
+    )
     global_ids = jnp.arange(coef_piece.shape[0])
     pick_map = (mid_flat[:, None] == global_ids[None, :]).astype(bf16)
     mid_picked = jnp.einsum("ik,krc->irc", pick_map, coef_piece, preferred_element_type=f32)

time: 169 us -> 239 us (1.41)
  waiting for transfers between devices: 0.72 us -> 97.6 us
  blocking collectives: 96.5 us -> 56 us
  matrix products: 16.8 us -> 23.4 us
  starting transfers between devices: 12.8 us -> 16 us
  local copies, waits for them, and re-layouts: 25.4 us -> 27.9 us
    ppermute x0 -> x15, waiting for transfers between devices: none -> 96.9 us  [product_in_turn(): arriving = lax.ppermute(held, axis, right) if step < length - 1 else None]
    all_gather x1 -> x0, blocking collectives: 57.8 us -> none  [shards(): lift_piece = lax.all_gather(mid_lift, 'leaf', axis=0, tiled=True)]
    all_gather x1, blocking collectives: 38.7 us -> 56 us  [shards(): coef_piece = lax.all_gather(mid_coef, 'leaf', axis=0, tiled=True)]
    dot_general x1 -> x16, matrix products: 0.4 us -> 5.34 us  [shards(): jnp.einsum('pk,krc->prc', lax.dynamic_slice_in_dim(group_map, offset, own...]
    ppermute x0 -> x15, starting transfers between devices: none -> 4.63 us  [product_in_turn(): arriving = lax.ppermute(held, axis, right) if step < length - 1 else None]
  transfers between devices with their start and end apart: 5 -> 20, of which waited for: 0 -> 14; matrix products, arithmetic and copies ran while one was open for 17% -> 16% of each run, Pallas kernels for 0% -> 0%
where the time goes in v1:
time: 239 us; the launch traced here: 238 us
  waiting for transfers between devices  97.6 us (41%)
  blocking collectives  56 us (23%)
  local copies, waits for them, and re-layouts  27.9 us (12%)
  matrix products  23.4 us (10%)
  starting transfers between devices  16 us (7%)
  between operations  14.1 us (6%)
  other arithmetic  2.97 us (1%)
    ppermute x15, waiting for transfers between devices, product_in_turn(): arriving = lax.ppermute(held, axis, right) if step < length - 1 else None  96.9 us
    all_gather x1, blocking collectives, shards(): coef_piece = lax.all_gather(mid_coef, 'leaf', axis=0, tiled=True)  56 us
    gather x2, local copies, waits for them, and re-layouts, shards(): picked = blocks[near_local]  18.7 us
    dot_general x1, matrix products, shards(): jnp.einsum('lsij,lsjc->lic', all_tiles, picked, preferred_element_type=f32)  12.7 us
    ppermute x2, starting transfers between devices, padded(): before = lax.ppermute(last, axis, up)  8.74 us
    dot_general x16, matrix products, shards(): jnp.einsum('pk,krc->prc', lax.dynamic_slice_in_dim(group_map, offset, own...  5.34 us
  transfers between devices with their start and end apart: 20, of which 14 were waited for; matrix products, arithmetic and copies ran while one was open for 16% of the time, Pallas kernels for 0%

profile of v1, /device:TPU:0, one launch (start us, length us, event | category | flops | bytes accessed | tf_op | source)
XLA Modules:
  0.0 237.9 jit_solution(7732027248855110284)
XLA Ops:
  6.6 0.7 all-gather.2.cloned.1.call-update
  7.3 0.3 copy-done
  7.6 0.3 copy-done.1
  7.9 0.3 convolution_convert_fusion
  8.6 3.0 %collective-permute-start.4 = (bf16[2,64,128]{2,1,0:T(8,128)(2,1)S(1)}, bf16[2,64,128]{2,1,0:T(8,128)(2,1)S(1)}, u32[]{:S(2)}, u32[]{:S(2)}) collective-permute-start(bf16[2,64,128]{2,1,0:T(8,128)(2,1)S(1)} %fusion.13), channel_id=1, source_target_pairs={{0,2},{2,4},{4,6},{6,8},{8,10},{10,12},{12,14},{14,16},{16,18},{18... | collective-permute-start | bytes 98312 | tf_op jit(solution)/shard_map/ppermute | solution.py:15
  11.6 3.4 %collective-permute-start.2 = (bf16[8,64,128]{2,1,0:T(8,128)(2,1)S(1)}, bf16[8,64,128]{2,1,0:T(8,128)(2,1)S(1)}, u32[]{:S(2)}, u32[]{:S(2)}) collective-permute-start(bf16[8,64,128]{2,1,0:T(8,128)(2,1)S(1)} %get-tuple-element.7), channel_id=1, source_target_pairs={{0,2},{2,4},{4,6},{6,8},{8,10},{10,12},{12,14},{14,16},{16,18},{18... | collective-permute-start | bytes 393224 | tf_op jit(solution)/shard_map/ppermute | solution.py:29
  15.0 1.3 collective-permute-start.3
  16.3 1.0 fusion.79
  17.3 5.3 %collective-permute-start = (bf16[2048,128]{1,0:T(8,128)(2,1)}, bf16[2048,128]{1,0:T(8,128)(2,1)}, u32[]{:S(2)}, u32[]{:S(2)}) collective-permute-start(bf16[2048,128]{1,0:T(8,128)(2,1)} %get-tuple-element.5), channel_id=1, source_target_pairs={{0,2},{2,4},{4,6},{6,8},{8,10},{10,12},{12,14},{14,16},{16,18},{18... | collective-permute-start | bytes 1572872 | tf_op jit(solution)/shard_map/ppermute | solution.py:29
  22.7 1.3 collective-permute-start.1
  24.7 0.2 fusion.38
  25.0 56.0 %all_gather.7 = bf16[32,64,128]{2,1,0:T(8,128)(2,1)S(1)} all-gather(bf16[2,64,128]{2,1,0:T(8,128)(2,1)S(1)} %bitcast.104), channel_id=1, replica_groups=mesh['leaf'=16,'col'=2] {'leaf'}, dimensions={0}, use_global_device_ids=true | all-gather | bytes 557056 | tf_op jit(solution)/shard_map/all_gather | solution.py:84
  81.0 0.4 convolution_convert_fusion.1
  81.7 0.7 broadcast_in_dim.60
  82.4 0.7 copy.61
  83.1 1.2 gather_fusion.2
  84.3 1.6 collective-permute-start.5
  86.1 5.6 %collective-permute-done.5 = bf16[2,64,128]{2,1,0:T(8,128)(2,1)S(1)} collective-permute-done((bf16[2,64,128]{2,1,0:T(8,128)(2,1)S(1)}, bf16[2,64,128]{2,1,0:T(8,128)(2,1)S(1)}, u32[]{:S(2)}, u32[]{:S(2)}) %collective-permute-start.5) | collective-permute-done | bytes 32800 | tf_op jit(solution)/shard_map/ppermute | solution.py:15
  92.0 7.3 %collective-permute-done.6 = bf16[2,64,128]{2,1,0:T(8,128)(2,1)S(1)} collective-permute-done((bf16[2,64,128]{2,1,0:T(8,128)(2,1)S(1)}, bf16[2,64,128]{2,1,0:T(8,128)(2,1)S(1)}, u32[]{:S(2)}, u32[]{:S(2)}) %collective-permute-start.6) | collective-permute-done | bytes 32800 | tf_op jit(solution)/shard_map/ppermute | solution.py:15
  99.5 7.4 %collective-permute-done.7 = bf16[2,64,128]{2,1,0:T(8,128)(2,1)} collective-permute-done((bf16[2,64,128]{2,1,0:T(8,128)(2,1)S(1)}, bf16[2,64,128]{2,1,0:T(8,128)(2,1)}, u32[]{:S(2)}, u32[]{:S(2)}) %collective-permute-start.7) | collective-permute-done | bytes 32800 | tf_op jit(solution)/shard_map/ppermute | solution.py:15
  106.9 1.0 convolution_add_fusion.11
  108.0 0.6 copy-done.6
  108.6 1.0 pad_maximum_fusion.1
  109.7 0.7 gather_fusion.1
  110.4 4.3 %collective-permute-done.8 = bf16[2,64,128]{2,1,0:T(8,128)(2,1)} collective-permute-done((bf16[2,64,128]{2,1,0:T(8,128)(2,1)}, bf16[2,64,128]{2,1,0:T(8,128)(2,1)}, u32[]{:S(2)}, u32[]{:S(2)}) %collective-permute-start.8) | collective-permute-done | bytes 32800 | tf_op jit(solution)/shard_map/ppermute | solution.py:15
  114.7 1.0 convolution_add_fusion.10
  115.8 6.7 %collective-permute-done.9 = bf16[2,64,128]{2,1,0:T(8,128)(2,1)S(1)} collective-permute-done((bf16[2,64,128]{2,1,0:T(8,128)(2,1)}, bf16[2,64,128]{2,1,0:T(8,128)(2,1)S(1)}, u32[]{:S(2)}, u32[]{:S(2)}) %collective-permute-start.9) | collective-permute-done | bytes 32800 | tf_op jit(solution)/shard_map/ppermute | solution.py:15
  122.7 7.3 %collective-permute-done.10 = bf16[2,64,128]{2,1,0:T(8,128)(2,1)S(1)} collective-permute-done((bf16[2,64,128]{2,1,0:T(8,128)(2,1)S(1)}, bf16[2,64,128]{2,1,0:T(8,128)(2,1)S(1)}, u32[]{:S(2)}, u32[]{:S(2)}) %collective-permute-start.10) | collective-permute-done | bytes 32800 | tf_op jit(solution)/shard_map/ppermute | solution.py:15
  130.2 7.3 %collective-permute-done.11 = bf16[2,64,128]{2,1,0:T(8,128)(2,1)S(1)} collective-permute-done((bf16[2,64,128]{2,1,0:T(8,128)(2,1)S(1)}, bf16[2,64,128]{2,1,0:T(8,128)(2,1)S(1)}, u32[]{:S(2)}, u32[]{:S(2)}) %collective-permute-start.11) | collective-permute-done | bytes 32800 | tf_op jit(solution)/shard_map/ppermute | solution.py:15
  137.7 7.3 %collective-permute-done.12 = bf16[2,64,128]{2,1,0:T(8,128)(2,1)S(1)} collective-permute-done((bf16[2,64,128]{2,1,0:T(8,128)(2,1)S(1)}, bf16[2,64,128]{2,1,0:T(8,128)(2,1)S(1)}, u32[]{:S(2)}, u32[]{:S(2)}) %collective-permute-start.12) | collective-permute-done | bytes 32800 | tf_op jit(solution)/shard_map/ppermute | solution.py:15
  145.0 0.2 convolution_add_fusion.6
  145.2 7.3 %collective-permute-done.13 = bf16[2,64,128]{2,1,0:T(8,128)(2,1)S(1)} collective-permute-done((bf16[2,64,128]{2,1,0:T(8,128)(2,1)S(1)}, bf16[2,64,128]{2,1,0:T(8,128)(2,1)S(1)}, u32[]{:S(2)}, u32[]{:S(2)}) %collective-permute-start.13) | collective-permute-done | bytes 32800 | tf_op jit(solution)/shard_map/ppermute | solution.py:15
  152.5 0.2 convolution_add_fusion.5
  152.7 7.3 %collective-permute-done.14 = bf16[2,64,128]{2,1,0:T(8,128)(2,1)S(1)} collective-permute-done((bf16[2,64,128]{2,1,0:T(8,128)(2,1)S(1)}, bf16[2,64,128]{2,1,0:T(8,128)(2,1)S(1)}, u32[]{:S(2)}, u32[]{:S(2)}) %collective-permute-start.14) | collective-permute-done | bytes 32800 | tf_op jit(solution)/shard_map/ppermute | solution.py:15
  160.3 7.5 %collective-permute-done.15 = bf16[2,64,128]{2,1,0:T(8,128)(2,1)S(1)} collective-permute-done((bf16[2,64,128]{2,1,0:T(8,128)(2,1)S(1)}, bf16[2,64,128]{2,1,0:T(8,128)(2,1)S(1)}, u32[]{:S(2)}, u32[]{:S(2)}) %collective-permute-start.15) | collective-permute-done | bytes 32800 | tf_op jit(solution)/shard_map/ppermute | solution.py:15
  168.0 7.3 %collective-permute-done.16 = bf16[2,64,128]{2,1,0:T(8,128)(2,1)S(1)} collective-permute-done((bf16[2,64,128]{2,1,0:T(8,128)(2,1)S(1)}, bf16[2,64,128]{2,1,0:T(8,128)(2,1)S(1)}, u32[]{:S(2)}, u32[]{:S(2)}) %collective-permute-start.16) | collective-permute-done | bytes 32800 | tf_op jit(solution)/shard_map/ppermute | solution.py:15
  175.5 7.3 %collective-permute-done.17 = bf16[2,64,128]{2,1,0:T(8,128)(2,1)S(1)} collective-permute-done((bf16[2,64,128]{2,1,0:T(8,128)(2,1)S(1)}, bf16[2,64,128]{2,1,0:T(8,128)(2,1)S(1)}, u32[]{:S(2)}, u32[]{:S(2)}) %collective-permute-start.17) | collective-permute-done | bytes 32800 | tf_op jit(solution)/shard_map/ppermute | solution.py:15
  182.8 0.2 convolution_add_fusion.1
  183.1 7.3 %collective-permute-done.18 = bf16[2,64,128]{2,1,0:T(8,128)(2,1)S(1)} collective-permute-done((bf16[2,64,128]{2,1,0:T(8,128)(2,1)S(1)}, bf16[2,64,128]{2,1,0:T(8,128)(2,1)S(1)}, u32[]{:S(2)}, u32[]{:S(2)}) %collective-permute-start.18) | collective-permute-done | bytes 32800 | tf_op jit(solution)/shard_map/ppermute | solution.py:15
  190.3 0.2 fusion.10
  190.6 1.2 fusion.12
  191.8 1.2 convolution_bitcast_fusion.1
  193.2 1.9 fusion.9
  195.2 1.7 pad_maximum_fusion
  196.8 6.6 %gather_fusion = bf16[128,256,128]{2,1,0:T(8,128)(2,1)} fusion(bf16[32,256,128]{2,1,0:T(8,128)(2,1)S(1)} %bitcast.97, s32[1024]{0:T(1024)S(1)} %pad_clamp_fusion.2), kind=kCustom, calls=%fused_computation | custom fusion | bytes 16777728 | tf_op jit(solution)/shard_map/gather | solution.py:65
  203.4 12.1 %copy.58 = bf16[128,256,128]{1,2,0:T(8,128)(2,1)} copy(bf16[128,256,128]{2,1,0:T(8,128)(2,1)} %gather_fusion) | data formatting | bytes 16777216 | tf_op jit(solution)/shard_map/gather | solution.py:65
  215.5 12.7 %fusion.4 = f32[16,256,128]{1,2,0:T(8,128)} fusion(f32[16,128,256]{2,1,0:T(8,128)S(1)} %copy-done.2, bf16[16,8,256,256]{3,2,1,0:T(8,128)(2,1)} %all-gather.2.cloned.1.call-done, bf16[16,8,256,128]{2,3,1,0:T(8,128)(2,1)} %bitcast.99, pred[16,8]{1,0:T(8,128)(4,1)S(1)} %iota_compare_fusion.1), kind=kOutput, calls=%fused_computation.9 | convolution fusion | flops 2152202240 | bytes 29360256 | tf_op jit(solution)/shard_map/lsij,lsjc->lic/dot_general | solution.py:68
  228.2 2.9 %copy.81 = f32[16,256,128]{2,1,0:T(8,128)} copy(f32[16,256,128]{1,2,0:T(8,128)} %fusion.4) | data formatting | bytes 4194304 | tf_op jit(solution)/shard_map/add | solution.py:129
  (78 shorter events, 3.6 us)
Async XLA Ops:
  6.5 1.0 copy-start
  6.5 1.4 copy-start.1
  6.5 1.7 copy-start.4
  6.5 1.9 copy-start.8
  6.5 208.9 %all-gather.2.cloned.1.call-start = ((), (), s32[]{:S(2)}) async-start(), calls=%async_computation | async-start | bytes 25165824 | tf_op jit(solution)/shard_map/all_gather | solution.py:62
  7.3 16.7 %copy-start.14 = (s32[2,4]{1,0:T(2,128)S(1)}, s32[2,4]{1,0:T(2,128)}, u32[]{:S(2)}) copy-start(s32[2,4]{1,0:T(2,128)} %param.21) | copy-start | bytes 100
  7.3 16.8 %copy-start.11 = (s32[16,4]{0,1:T(4,128)S(1)}, s32[16,4]{0,1:T(4,128)}, u32[]{:S(2)}) copy-start(s32[16,4]{0,1:T(4,128)} %param.18) | copy-start | bytes 772
  7.3 16.9 %copy-start.10 = (s32[16,8]{0,1:T(8,128)S(1)}, s32[16,8]{0,1:T(8,128)}, u32[]{:S(2)}) copy-start(s32[16,8]{0,1:T(8,128)} %param.14) | copy-start | bytes 1540
  7.3 17.3 %copy-start.13 = (s32[16]{0:T(128)S(1)}, s32[16]{0:T(128)}, u32[]{:S(2)}) copy-start(s32[16]{0:T(128)} %param.15) | copy-start | bytes 196
  7.3 75.8 %copy-start.9 = (bf16[4,64,256]{2,1,0:T(8,128)(2,1)S(1)}, bf16[4,64,256]{2,1,0:T(8,128)(2,1)}, u32[]{:S(2)}) copy-start(bf16[4,64,256]{2,1,0:T(8,128)(2,1)} %param.23) | copy-start | bytes 393220
  8.6 75.7 %collective-permute-start.4 = (bf16[2,64,128]{2,1,0:T(8,128)(2,1)S(1)}, bf16[2,64,128]{2,1,0:T(8,128)(2,1)S(1)}, u32[]{:S(2)}, u32[]{:S(2)}) collective-permute-start(bf16[2,64,128]{2,1,0:T(8,128)(2,1)S(1)} %fusion.13), channel_id=1, source_target_pairs={{0,2},{2,4},{4,6},{6,8},{8,10},{10,12},{12,14},{14,16},{16,18},{18... | collective-permute-start | bytes 98312 | tf_op jit(solution)/shard_map/ppermute | solution.py:15
  11.6 96.4 %collective-permute-start.2 = (bf16[8,64,128]{2,1,0:T(8,128)(2,1)S(1)}, bf16[8,64,128]{2,1,0:T(8,128)(2,1)S(1)}, u32[]{:S(2)}, u32[]{:S(2)}) collective-permute-start(bf16[8,64,128]{2,1,0:T(8,128)(2,1)S(1)} %get-tuple-element.7), channel_id=1, source_target_pairs={{0,2},{2,4},{4,6},{6,8},{8,10},{10,12},{12,14},{14,16},{16,18},{18... | collective-permute-start | bytes 393224 | tf_op jit(solution)/shard_map/ppermute | solution.py:29
  15.0 93.6 %collective-permute-start.3 = (bf16[8,64,128]{2,1,0:T(8,128)(2,1)S(1)}, bf16[8,64,128]{2,1,0:T(8,128)(2,1)}, u32[]{:S(2)}, u32[]{:S(2)}) collective-permute-start(bf16[8,64,128]{2,1,0:T(8,128)(2,1)S(1)} %get-tuple-element.8), channel_id=1, source_target_pairs={{2,0},{4,2},{6,4},{8,6},{10,8},{12,10},{14,12},{16,14},{18,16},{20... | collective-permute-start | bytes 393224 | tf_op jit(solution)/shard_map/ppermute | solution.py:30
  17.3 177.8 %collective-permute-start = (bf16[2048,128]{1,0:T(8,128)(2,1)}, bf16[2048,128]{1,0:T(8,128)(2,1)}, u32[]{:S(2)}, u32[]{:S(2)}) collective-permute-start(bf16[2048,128]{1,0:T(8,128)(2,1)} %get-tuple-element.5), channel_id=1, source_target_pairs={{0,2},{2,4},{4,6},{6,8},{8,10},{10,12},{12,14},{14,16},{16,18},{18... | collective-permute-start | bytes 1572872 | tf_op jit(solution)/shard_map/ppermute | solution.py:29
  22.7 172.5 %collective-permute-start.1 = (bf16[2048,128]{1,0:T(8,128)(2,1)}, bf16[2048,128]{1,0:T(8,128)(2,1)}, u32[]{:S(2)}, u32[]{:S(2)}) collective-permute-start(bf16[2048,128]{1,0:T(8,128)(2,1)} %get-tuple-element.6), channel_id=1, source_target_pairs={{2,0},{4,2},{6,4},{8,6},{10,8},{12,10},{14,12},{16,14},{18,16},{20... | collective-permute-start | bytes 1572872 | tf_op jit(solution)/shard_map/ppermute | solution.py:30
  84.3 7.5 %collective-permute-start.5 = (bf16[2,64,128]{2,1,0:T(8,128)(2,1)S(1)}, bf16[2,64,128]{2,1,0:T(8,128)(2,1)S(1)}, u32[]{:S(2)}, u32[]{:S(2)}) collective-permute-start(bf16[2,64,128]{2,1,0:T(8,128)(2,1)S(1)} %collective-permute-done.4), channel_id=1, source_target_pairs={{0,2},{2,4},{4,6},{6,8},{8,10},{10,12},{12,14},{14,16},{16,18},{18... | collective-permute-start | bytes 98312 | tf_op jit(solution)/shard_map/ppermute | solution.py:15
  91.8 7.5 %collective-permute-start.6 = (bf16[2,64,128]{2,1,0:T(8,128)(2,1)S(1)}, bf16[2,64,128]{2,1,0:T(8,128)(2,1)S(1)}, u32[]{:S(2)}, u32[]{:S(2)}) collective-permute-start(bf16[2,64,128]{2,1,0:T(8,128)(2,1)S(1)} %collective-permute-done.5), channel_id=1, source_target_pairs={{0,2},{2,4},{4,6},{6,8},{8,10},{10,12},{12,14},{14,16},{16,18},{18... | collective-permute-start | bytes 98312 | tf_op jit(solution)/shard_map/ppermute | solution.py:15
  99.3 7.6 %collective-permute-start.7 = (bf16[2,64,128]{2,1,0:T(8,128)(2,1)S(1)}, bf16[2,64,128]{2,1,0:T(8,128)(2,1)}, u32[]{:S(2)}, u32[]{:S(2)}) collective-permute-start(bf16[2,64,128]{2,1,0:T(8,128)(2,1)S(1)} %collective-permute-done.6), channel_id=1, source_target_pairs={{0,2},{2,4},{4,6},{6,8},{8,10},{10,12},{12,14},{14,16},{16,18},{18... | collective-permute-start | bytes 98312 | tf_op jit(solution)/shard_map/ppermute | solution.py:15
  106.9 7.8 %collective-permute-start.8 = (bf16[2,64,128]{2,1,0:T(8,128)(2,1)}, bf16[2,64,128]{2,1,0:T(8,128)(2,1)}, u32[]{:S(2)}, u32[]{:S(2)}) collective-permute-start(bf16[2,64,128]{2,1,0:T(8,128)(2,1)} %collective-permute-done.7), channel_id=1, source_target_pairs={{0,2},{2,4},{4,6},{6,8},{8,10},{10,12},{12,14},{14,16},{16,18},{18... | collective-permute-start | bytes 98312 | tf_op jit(solution)/shard_map/ppermute | solution.py:15
  107.9 82.7 %copy-start.7 = (bf16[2,64,256]{2,1,0:T(8,128)(2,1)S(1)}, bf16[2,64,256]{2,1,0:T(8,128)(2,1)}, u32[]{:S(2)}) copy-start(bf16[2,64,256]{2,1,0:T(8,128)(2,1)} %gather_fusion.2) | copy-start | bytes 196612
  107.9 85.3 %copy-start.3 = (bf16[16,64,256]{2,1,0:T(8,128)(2,1)S(1)}, bf16[16,64,256]{2,1,0:T(8,128)(2,1)}, u32[]{:S(2)}) copy-start(bf16[16,64,256]{2,1,0:T(8,128)(2,1)} %param.17) | copy-start | bytes 1572868
  108.0 0.6 copy-start.6
  108.6 82.0 %copy-start.12 = (pred[2,256]{1,0:T(4,128)(4,1)S(1)}, pred[2,256]{1,0:T(4,128)(4,1)}, u32[]{:S(2)}) copy-start(pred[2,256]{1,0:T(4,128)(4,1)} %broadcast_in_dim.60) | copy-start | bytes 1540
  109.7 82.1 %copy-start.5 = (bf16[8,64,128]{2,1,0:T(8,128)(2,1)S(1)}, bf16[8,64,128]{2,1,0:T(8,128)(2,1)}, u32[]{:S(2)}) copy-start(bf16[8,64,128]{2,1,0:T(8,128)(2,1)} %copy.61) | copy-start | bytes 393220
  114.7 7.7 %collective-permute-start.9 = (bf16[2,64,128]{2,1,0:T(8,128)(2,1)}, bf16[2,64,128]{2,1,0:T(8,128)(2,1)S(1)}, u32[]{:S(2)}, u32[]{:S(2)}) collective-permute-start(bf16[2,64,128]{2,1,0:T(8,128)(2,1)} %collective-permute-done.8), channel_id=1, source_target_pairs={{0,2},{2,4},{4,6},{6,8},{8,10},{10,12},{12,14},{14,16},{16,18},{18... | collective-permute-start | bytes 98312 | tf_op jit(solution)/shard_map/ppermute | solution.py:15
  122.4 7.5 %collective-permute-start.10 = (bf16[2,64,128]{2,1,0:T(8,128)(2,1)S(1)}, bf16[2,64,128]{2,1,0:T(8,128)(2,1)S(1)}, u32[]{:S(2)}, u32[]{:S(2)}) collective-permute-start(bf16[2,64,128]{2,1,0:T(8,128)(2,1)S(1)} %collective-permute-done.9), channel_id=1, source_target_pairs={{0,2},{2,4},{4,6},{6,8},{8,10},{10,12},{12,14},{14,16},{16,18},{18... | collective-permute-start | bytes 98312 | tf_op jit(solution)/shard_map/ppermute | solution.py:15
  130.0 7.5 %collective-permute-start.11 = (bf16[2,64,128]{2,1,0:T(8,128)(2,1)S(1)}, bf16[2,64,128]{2,1,0:T(8,128)(2,1)S(1)}, u32[]{:S(2)}, u32[]{:S(2)}) collective-permute-start(bf16[2,64,128]{2,1,0:T(8,128)(2,1)S(1)} %collective-permute-done.10), channel_id=1, source_target_pairs={{0,2},{2,4},{4,6},{6,8},{8,10},{10,12},{12,14},{14,16},{16,18},{18... | collective-permute-start | bytes 98312 | tf_op jit(solution)/shard_map/ppermute | solution.py:15
  137.5 7.5 %collective-permute-start.12 = (bf16[2,64,128]{2,1,0:T(8,128)(2,1)S(1)}, bf16[2,64,128]{2,1,0:T(8,128)(2,1)S(1)}, u32[]{:S(2)}, u32[]{:S(2)}) collective-permute-start(bf16[2,64,128]{2,1,0:T(8,128)(2,1)S(1)} %collective-permute-done.11), channel_id=1, source_target_pairs={{0,2},{2,4},{4,6},{6,8},{8,10},{10,12},{12,14},{14,16},{16,18},{18... | collective-permute-start | bytes 98312 | tf_op jit(solution)/shard_map/ppermute | solution.py:15
  145.0 7.5 %collective-permute-start.13 = (bf16[2,64,128]{2,1,0:T(8,128)(2,1)S(1)}, bf16[2,64,128]{2,1,0:T(8,128)(2,1)S(1)}, u32[]{:S(2)}, u32[]{:S(2)}) collective-permute-start(bf16[2,64,128]{2,1,0:T(8,128)(2,1)S(1)} %collective-permute-done.12), channel_id=1, source_target_pairs={{0,2},{2,4},{4,6},{6,8},{8,10},{10,12},{12,14},{14,16},{16,18},{18... | collective-permute-start | bytes 98312 | tf_op jit(solution)/shard_map/ppermute | solution.py:15
  152.5 7.5 %collective-permute-start.14 = (bf16[2,64,128]{2,1,0:T(8,128)(2,1)S(1)}, bf16[2,64,128]{2,1,0:T(8,128)(2,1)S(1)}, u32[]{:S(2)}, u32[]{:S(2)}) collective-permute-start(bf16[2,64,128]{2,1,0:T(8,128)(2,1)S(1)} %collective-permute-done.13), channel_id=1, source_target_pairs={{0,2},{2,4},{4,6},{6,8},{8,10},{10,12},{12,14},{14,16},{16,18},{18... | collective-permute-start | bytes 98312 | tf_op jit(solution)/shard_map/ppermute | solution.py:15
  160.0 7.8 %collective-permute-start.15 = (bf16[2,64,128]{2,1,0:T(8,128)(2,1)S(1)}, bf16[2,64,128]{2,1,0:T(8,128)(2,1)S(1)}, u32[]{:S(2)}, u32[]{:S(2)}) collective-permute-start(bf16[2,64,128]{2,1,0:T(8,128)(2,1)S(1)} %collective-permute-done.14), channel_id=1, source_target_pairs={{0,2},{2,4},{4,6},{6,8},{8,10},{10,12},{12,14},{14,16},{16,18},{18... | collective-permute-start | bytes 98312 | tf_op jit(solution)/shard_map/ppermute | solution.py:15
  167.8 7.5 %collective-permute-start.16 = (bf16[2,64,128]{2,1,0:T(8,128)(2,1)S(1)}, bf16[2,64,128]{2,1,0:T(8,128)(2,1)S(1)}, u32[]{:S(2)}, u32[]{:S(2)}) collective-permute-start(bf16[2,64,128]{2,1,0:T(8,128)(2,1)S(1)} %collective-permute-done.15), channel_id=1, source_target_pairs={{0,2},{2,4},{4,6},{6,8},{8,10},{10,12},{12,14},{14,16},{16,18},{18... | collective-permute-start | bytes 98312 | tf_op jit(solution)/shard_map/ppermute | solution.py:15
  175.3 7.5 %collective-permute-start.17 = (bf16[2,64,128]{2,1,0:T(8,128)(2,1)S(1)}, bf16[2,64,128]{2,1,0:T(8,128)(2,1)S(1)}, u32[]{:S(2)}, u32[]{:S(2)}) collective-permute-start(bf16[2,64,128]{2,1,0:T(8,128)(2,1)S(1)} %collective-permute-done.16), channel_id=1, source_target_pairs={{0,2},{2,4},{4,6},{6,8},{8,10},{10,12},{12,14},{14,16},{16,18},{18... | collective-permute-start | bytes 98312 | tf_op jit(solution)/shard_map/ppermute | solution.py:15
  182.8 7.5 %collective-permute-start.18 = (bf16[2,64,128]{2,1,0:T(8,128)(2,1)S(1)}, bf16[2,64,128]{2,1,0:T(8,128)(2,1)S(1)}, u32[]{:S(2)}, u32[]{:S(2)}) collective-permute-start(bf16[2,64,128]{2,1,0:T(8,128)(2,1)S(1)} %collective-permute-done.17), channel_id=1, source_target_pairs={{0,2},{2,4},{4,6},{6,8},{8,10},{10,12},{12,14},{14,16},{16,18},{18... | collective-permute-start | bytes 98312 | tf_op jit(solution)/shard_map/ppermute | solution.py:15
  203.4 12.1 %copy-start.2 = (f32[16,128,256]{2,1,0:T(8,128)S(1)}, f32[16,128,256]{2,1,0:T(8,128)}, u32[]{:S(2)}) copy-start(f32[16,128,256]{2,1,0:T(8,128)} %fusion.9) | copy-start | bytes 6291460
Sparse Core Ops, SparseCore 0:
  8.9 32.7 all-gather.1
